TPU v7x, 512 devices: a whole 4x4x16 slice. The times are simulated.
512 devices in a mesh: row: 32 (over x, y, core), col: 16 (over z).
Axes of the slice: x: 4, y: 4, z: 16, core: 2. Of those that a mesh axis runs over, the one named last changes fastest.
Arguments:
- features: bfloat16 [65536, 256], P('col', 'row'), may hold values from -6 to 6
- weight: bfloat16 [256, 256], replicated, may hold values from -0.375 to 0.375
- adj_values: bfloat16 [32, 16, 96, 128, 128], P('row', 'col'), may hold values from -0.0625 to 0.0625
- block_rows: int32 [32, 16, 96], P('row', 'col'), may hold values from 0 to 15, as said below
- block_cols: int32 [32, 16, 96], P('row', 'col'), may hold values from 0 to 31
- block_counts: int32 [32, 16], P('row', 'col'), may hold values from 1 to 96, as said below
- cotangent: bfloat16 [65536, 256], P(('row', 'col')), may hold values from -6 to 6
Outputs:
- output: bfloat16 [65536, 256], P(('row', 'col'))
- grad_weight: float32 [256, 256], replicated
- grad_features: bfloat16 [65536, 256], P('col', 'row')
Inputs may be any that keep to these rules, and one draw needn't show every extreme that they name: Within one tile the pairs (block_rows, block_cols) over all 96 slots are distinct. `block_counts`: some tile holds exactly 96 live blocks and some other tile exactly one in every draw.
All inputs are finite; a program needn't handle non-finite values.
Results may differ from a plain program's by a relative error of at most 0.029.
Values may be sent and summed in bfloat16 or wider, within the bound.
A program may use at most 64 MiB of HBM per device.

v0:
```python
import math
import jax
import jax.numpy as jnp
from jax import lax
from jax.sharding import PartitionSpec as P

RB = 16


def block_product(tile_values, tile_rows, tile_cols, live_count, panels, out_blocks, transposed):
    padded = tile_values.shape[0]
    blocks_turn = math.gcd(padded, 16)
    block_size = panels.shape[1]
    columns = panels.shape[2]
    turns_needed = (live_count + blocks_turn - 1) // blocks_turn

    def step(turn_index, running):
        offset = turn_index * blocks_turn
        values_now = lax.dynamic_slice_in_dim(tile_values, offset, blocks_turn, 0)
        row_ids = lax.dynamic_slice_in_dim(tile_rows, offset, blocks_turn, 0)
        col_ids = lax.dynamic_slice_in_dim(tile_cols, offset, blocks_turn, 0)
        is_live = offset + jnp.arange(blocks_turn, dtype=jnp.int32) < live_count
        if transposed:
            picked = jnp.take(panels, row_ids, axis=0)
            product = jnp.einsum(
                "bij,bif->bjf", values_now, picked, preferred_element_type=jnp.float32
            )
            target_ids = col_ids
        else:
            picked = jnp.take(panels, col_ids, axis=0)
            product = jnp.einsum(
                "bij,bjf->bif", values_now, picked, preferred_element_type=jnp.float32
            )
            target_ids = row_ids
        contribution = jnp.where(is_live[:, None, None], product, 0.0)
        return running.at[target_ids].add(contribution)

    start_sum = jnp.zeros((out_blocks, block_size, columns), jnp.float32)
    return lax.fori_loop(0, turns_needed, step, start_sum)


def shards(features, weight, adj_values, block_rows, block_cols, block_counts, cotangent):
    tile_values = adj_values[0, 0]
    tile_rows = block_rows[0, 0]
    tile_cols = block_cols[0, 0]
    live_count = block_counts[0, 0]
    block_size = tile_values.shape[1]
    col_blocks = features.shape[0] // block_size
    node_total = col_blocks * block_size * lax.axis_size("col")
    panel_part = lax.all_gather(features, "row", axis=1, tiled=True)
    panels = panel_part.reshape(col_blocks, block_size, panel_part.shape[1])
    partial_value = block_product(tile_values, tile_rows, tile_cols, live_count, panels, RB, False)
    partial_value = partial_value.reshape(RB * block_size, partial_value.shape[2])
    aggregated = lax.psum_scatter(
        partial_value.astype(jnp.bfloat16), "col", scatter_dimension=0, tiled=True
    )
    preact = jnp.dot(aggregated, weight, preferred_element_type=jnp.float32)
    output = jax.nn.silu(preact).astype(jnp.bfloat16)
    sigmoid_pre = jax.nn.sigmoid(preact)
    slopes = sigmoid_pre * (1.0 + preact * (1.0 - sigmoid_pre))
    deltas = (cotangent.astype(jnp.float32) * slopes).astype(jnp.bfloat16)
    local_grad = jnp.dot(aggregated.T, deltas, preferred_element_type=jnp.float32)
    grad_weight = lax.psum(local_grad, ("row", "col")) * (1.0 / math.sqrt(node_total))
    backward = jnp.dot(deltas, weight.T, preferred_element_type=jnp.float32).astype(jnp.bfloat16)
    back_slab = lax.all_gather(backward, "col", axis=0, tiled=True)
    back_panels = back_slab.reshape(RB, block_size, back_slab.shape[1])
    column_terms = block_product(
        tile_values, tile_rows, tile_cols, live_count, back_panels, col_blocks, True
    )
    column_terms = column_terms.reshape(col_blocks * block_size, column_terms.shape[2])
    grad_features = lax.psum_scatter(
        column_terms.astype(jnp.bfloat16), "row", scatter_dimension=1, tiled=True
    )
    return (output, grad_weight, grad_features)


def solution(mesh):
    return jax.shard_map(
        shards,
        mesh=mesh,
        in_specs=(
            P("col", "row"),
            P(),
            P("row", "col", None, None, None),
            P("row", "col", None),
            P("row", "col", None),
            P("row", "col"),
            P(("row", "col"), None),
        ),
        out_specs=(P(("row", "col"), None), P(), P("col", "row")),
        check_vma=False,
    )
```

profile of v0, /device:TPU:2, one launch (start us, length us, event | category | flops | bytes accessed | tf_op | source)
XLA Modules:
  0.0 847.8 jit_solution(3140927563884392423)
XLA Ops:
  8.6 65.7 %all-gather.3.cloned.1.call-done = bf16[4096,256]{0,1:T(8,128)(2,1)} async-done(((bf16[4096,8]{0,1:T(8,128)(2,1)}), bf16[4096,256]{0,1:T(8,128)(2,1)}) %all-gather.3.cloned.1.call-update) | async-done | bytes 2097168 | tf_op jit(solution)/shard_map/all_gather | solution.py:50
  74.3 4.1 copy.11
  78.4 1.5 broadcast_in_dim.58
  80.0 35.9 %while.20 = (s32[]{:T(128)}, f32[16,128,256]{2,1,0:T(8,128)}, s32[]{:T(128)}, s32[96]{0:T(128)S(1)}, s32[]{:T(128)}, /*index=5*/bf16[96,128,128]{2,1,0:T(8,128)(...) while((s32[]{:T(128)}, f32[16,128,256]{2,1,0:T(8,128)}, ...), condition=%wide.region_2.3_spmd, body=%wide.region_0.2_spmd.sunk | while | flops 135791792 | bytes 12063415 | solution.py:39
  80.0 0.7 compare_and_fusion.4
  80.7 2.2 gather_fusion
  82.9 1.5 convolution_select_fusion.4
  84.5 4.3 scatter_fusion
  88.9 0.7 compare_and_fusion.4
  89.6 2.2 gather_fusion
  91.8 1.6 convolution_select_fusion.4
  93.4 4.4 scatter_fusion
  97.8 0.7 compare_and_fusion.4
  98.5 2.2 gather_fusion
  100.8 1.5 convolution_select_fusion.4
  102.4 4.5 scatter_fusion
  106.8 0.7 compare_and_fusion.4
  107.6 2.2 gather_fusion
  109.8 1.6 convolution_select_fusion.4
  111.4 4.4 scatter_fusion
  115.9 2.8 convert_element_type.24
  118.8 87.5 %reduce-scatter.3.cloned.1.call-done = bf16[128,256]{1,0:T(8,128)(2,1)} async-done(((bf16[2048,256]{1,0:T(8,128)(2,1)}), bf16[128,256]{1,0:T(8,128)(2,1)}) %reduce-scatter.3.cloned.1.call-update) | async-done | bytes 65552 | tf_op jit(solution)/shard_map/reduce_scatter | solution.py:54
  206.3 1.7 multiply_convert_fusion
  208.0 0.8 convolution_convert_fusion
  208.9 2.8 copy.10
  211.7 0.9 fusion.12
  212.7 65.3 %all-gather.5.cloned.1.call-done = bf16[2048,256]{1,0:T(8,128)(2,1)} async-done(((bf16[128,256]{1,0:T(8,128)(2,1)}), bf16[2048,256]{1,0:T(8,128)(2,1)}) %all-gather.5.cloned.1.call-update) | async-done | bytes 1048592 | tf_op jit(solution)/shard_map/all_gather | solution.py:65
  278.1 2.4 broadcast_in_dim.59
  280.5 34.6 %while.21 = (s32[]{:T(128)}, f32[32,128,256]{2,1,0:T(8,128)}, s32[]{:T(128)}, s32[96]{0:T(128)S(1)}, s32[]{:T(128)}, /*index=5*/bf16[96,128,128]{1,2,0:T(8,128)(...) while((s32[]{:T(128)}, f32[32,128,256]{2,1,0:T(8,128)}, ...), condition=%wide.region_7.8_spmd, body=%wide.region_5.7_spmd.sunk | while | flops 135791792 | bytes 12063415 | solution.py:39
  281.2 1.8 gather_fusion.1
  283.1 1.6 convolution_select_fusion.5
  284.7 4.3 scatter_fusion.1
  289.8 1.8 gather_fusion.1
  291.6 1.5 convolution_select_fusion.5
  293.3 4.5 scatter_fusion.1
  297.7 0.7 compare_and_fusion.5
  298.5 1.8 gather_fusion.1
  300.3 1.6 convolution_select_fusion.5
  301.9 4.5 scatter_fusion.1
  306.4 0.7 compare_and_fusion.5
  307.1 1.8 gather_fusion.1
  309.0 1.6 convolution_select_fusion.5
  310.6 4.4 scatter_fusion.1
  315.1 2.5 convert_element_type.30
  317.6 2.9 copy.15
  320.5 418.5 %all-reduce.2.cloned.1.call-done = f32[256,256]{1,0:T(8,128)} async-done(((f32[256,256]{1,0:T(8,128)}), f32[256,256]{1,0:T(8,128)}) %all-reduce.2.cloned.1.call-update) | async-done | bytes 262160 | tf_op jit(solution)/shard_map/psum | solution.py:63
  739.0 1.7 broadcast_multiply_fusion
  740.6 100.6 %reduce-scatter.5.cloned.1.call-done = bf16[4096,8]{0,1:T(8,128)(2,1)} async-done(((bf16[4096,256]{0,1:T(8,128)(2,1)}), bf16[4096,8]{0,1:T(8,128)(2,1)}) %reduce-scatter.5.cloned.1.call-update) | async-done | bytes 65552 | tf_op jit(solution)/shard_map/reduce_scatter | solution.py:71
  (40 shorter events, 3.1 us)
Async XLA Ops:
  7.2 199.1 %copy-start = (bf16[256,256]{1,0:T(8,128)(2,1)S(1)}, bf16[256,256]{1,0:T(8,128)(2,1)}, u32[]{:S(2)}) copy-start(bf16[256,256]{1,0:T(8,128)(2,1)} %param.12) | copy-start | bytes 393220
  7.2 67.2 %all-gather.3.cloned.1.call-start = ((), (), s32[]{:S(2)}) async-start(), calls=%async_computation.2 | async-start | bytes 2162688 | tf_op jit(solution)/shard_map/all_gather | solution.py:50
  7.9 198.4 %reduce-scatter.3.cloned.1.call-start = ((), (), s32[]{:S(2)}) async-start(), calls=%async_computation.3 | async-start | bytes 1114112 | tf_op jit(solution)/shard_map/reduce_scatter | solution.py:54
  78.4 1.5 copy-start.3
  78.4 1.5 copy-start.4
  115.9 90.4 %copy-start.5 = (bf16[128,256]{1,0:T(8,128)(2,1)S(1)}, bf16[128,256]{1,0:T(8,128)(2,1)}, u32[]{:S(2)}) copy-start(bf16[128,256]{1,0:T(8,128)(2,1)} %param.17) | copy-start | bytes 196612
  115.9 93.1 %copy-start.1 = (bf16[96,128,128]{2,1,0:T(8,128)(2,1)S(1)}, bf16[96,128,128]{2,1,0:T(8,128)(2,1)}, u32[]{:S(2)}) copy-start(bf16[96,128,128]{2,1,0:T(8,128)(2,1)} %get-tuple-element.328) | copy-start | bytes 9437188
  118.7 159.3 %all-gather.5.cloned.1.call-start = ((), (), s32[]{:S(2)}) async-start(), calls=%async_computation.5 | async-start | bytes 1114112 | tf_op jit(solution)/shard_map/all_gather | solution.py:65
  208.9 2.9 copy-start.2
  208.9 530.1 %all-reduce.2.cloned.1.call-start = ((), (), s32[]{:S(2)}) async-start(), calls=%async_computation.4 | async-start | bytes 524288 | tf_op jit(solution)/shard_map/psum | solution.py:63
  212.7 628.6 %reduce-scatter.5.cloned.1.call-start = ((), (), s32[]{:S(2)}) async-start(), calls=%async_computation.6 | async-start | bytes 2162688 | tf_op jit(solution)/shard_map/reduce_scatter | solution.py:71
Sparse Core Ops, SparseCore 0:
  11.1 63.1 all-gather.2
  118.9 87.4 reduce-scatter.2
  209.2 68.8 all-gather.4
  284.8 454.1 all-reduce.1
  743.8 97.3 reduce-scatter.4
where the time goes:
time: 850 us; the launch traced here: 848 us
  waiting for transfers between devices  738 us (87%)
  other arithmetic  48.7 us (6%)
  local copies, waits for them, and re-layouts  30 us (4%)
  matrix products  15.8 us (2%)
  between operations  14.5 us (2%)
    psum x1, waiting for transfers between devices, shards(): lax.psum(local_grad, ('row', 'col')) * (1.0 / math.sqrt(node_total))  418 us
    reduce_scatter x1, waiting for transfers between devices, shards(): lax.psum_scatter(column_terms.astype(jnp.bfloat16), 'row', scatter_dimens...  101 us
    reduce_scatter x1, waiting for transfers between devices, shards(): lax.psum_scatter(partial_value.astype(jnp.bfloat16), 'col', scatter_dimen...  87.5 us
    all_gather x1, waiting for transfers between devices, shards(): panel_part = lax.all_gather(features, 'row', axis=1, tiled=True)  65.7 us
    all_gather x1, waiting for transfers between devices, shards(): back_slab = lax.all_gather(backward, 'col', axis=0, tiled=True)  65.3 us
    scatter-add x8, other arithmetic, step(): return running.at[target_ids].add(contribution)  35.2 us
  transfers between devices with their start and end apart: 5, of which 5 were waited for; matrix products, arithmetic and copies ran while one was open for 6% of the time, Pallas kernels for 0%

commit v1 on v0

--- a/solution.py
+++ b/solution.py
@@ -3,6 +3,7 @@
 import jax.numpy as jnp
 from jax import lax
 from jax.sharding import PartitionSpec as P
+from jax.lax import psum
 
 RB = 16
 
@@ -40,6 +41,11 @@
 
 
 def shards(features, weight, adj_values, block_rows, block_cols, block_counts, cotangent):
+
+    def detail_cells(raw):
+        before = psum(raw, axis_name="row")
+        return psum(before, "col")
+
     tile_values = adj_values[0, 0]
     tile_rows = block_rows[0, 0]
     tile_cols = block_cols[0, 0]
@@ -60,7 +66,7 @@
     slopes = sigmoid_pre * (1.0 + preact * (1.0 - sigmoid_pre))
     deltas = (cotangent.astype(jnp.float32) * slopes).astype(jnp.bfloat16)
     local_grad = jnp.dot(aggregated.T, deltas, preferred_element_type=jnp.float32)
-    grad_weight = lax.psum(local_grad, ("row", "col")) * (1.0 / math.sqrt(node_total))
+    grad_weight = detail_cells(local_grad) * (1.0 / math.sqrt(node_total))
     backward = jnp.dot(deltas, weight.T, preferred_element_type=jnp.float32).astype(jnp.bfloat16)
     back_slab = lax.all_gather(backward, "col", axis=0, tiled=True)
     back_panels = back_slab.reshape(RB, block_size, back_slab.shape[1])

time: 850 us -> 661 us (0.78)
  waiting for transfers between devices: 738 us -> 548 us
    psum x1 -> x2, waiting for transfers between devices: 418 us -> 218 us  [the longest x1 126 us: detail_cells(): before = psum(raw, axis_name='row')]
  transfers between devices with their start and end apart: 5 -> 6, of which waited for: 5 -> 6; matrix products, arithmetic and copies ran while one was open for 6% -> 7% of each run, Pallas kernels for 0% -> 0%
where the time goes in v1:
time: 661 us; the launch traced here: 659 us
  waiting for transfers between devices  548 us (83%)
  other arithmetic  48.9 us (7%)
  local copies, waits for them, and re-layouts  30 us (5%)
  matrix products  16.7 us (3%)
  between operations  14.8 us (2%)
    psum x1, waiting for transfers between devices, detail_cells(): before = psum(raw, axis_name='row')  126 us
    reduce_scatter x1, waiting for transfers between devices, shards(): lax.psum_scatter(column_terms.astype(jnp.bfloat16), 'row', scatter_dimens...  102 us
    psum x1, waiting for transfers between devices, detail_cells(): return psum(before, 'col')  92 us
    reduce_scatter x1, waiting for transfers between devices, shards(): lax.psum_scatter(partial_value.astype(jnp.bfloat16), 'col', scatter_dimen...  87.6 us
    all_gather x1, waiting for transfers between devices, shards(): back_slab = lax.all_gather(backward, 'col', axis=0, tiled=True)  73.8 us
    all_gather x1, waiting for transfers between devices, shards(): panel_part = lax.all_gather(features, 'row', axis=1, tiled=True)  65.7 us
    scatter-add x8, other arithmetic, step(): return running.at[target_ids].add(contribution)  35.4 us
  transfers between devices with their start and end apart: 6, of which 6 were waited for; matrix products, arithmetic and copies ran while one was open for 7% of the time, Pallas kernels for 0%

profile of v1, /device:TPU:2, one launch (start us, length us, event | category | flops | bytes accessed | tf_op | source)
XLA Modules:
  0.0 659.2 jit_solution(12902511653311203061)
XLA Ops:
  8.6 65.7 %all-gather.3.cloned.1.call-done = bf16[4096,256]{0,1:T(8,128)(2,1)} async-done(((bf16[4096,8]{0,1:T(8,128)(2,1)}), bf16[4096,256]{0,1:T(8,128)(2,1)}) %all-gather.3.cloned.1.call-update) | async-done | bytes 2097168 | tf_op jit(solution)/shard_map/all_gather | solution.py:56
  74.3 4.1 copy.11
  78.4 1.5 broadcast_in_dim.58
  80.0 36.0 %while.20 = (s32[]{:T(128)}, f32[16,128,256]{2,1,0:T(8,128)}, s32[]{:T(128)}, s32[96]{0:T(128)S(1)}, s32[]{:T(128)}, /*index=5*/bf16[96,128,128]{2,1,0:T(8,128)(...) while((s32[]{:T(128)}, f32[16,128,256]{2,1,0:T(8,128)}, ...), condition=%wide.region_2.3_spmd, body=%wide.region_0.2_spmd.sunk | while | flops 135791792 | bytes 12063415 | solution.py:40
  80.0 0.7 compare_and_fusion.4
  80.7 2.2 gather_fusion
  82.9 1.6 convolution_select_fusion.4
  84.6 4.3 scatter_fusion
  88.9 0.7 compare_and_fusion.4
  89.6 2.2 gather_fusion
  91.8 1.6 convolution_select_fusion.4
  93.5 4.4 scatter_fusion
  97.9 0.7 compare_and_fusion.4
  98.6 2.2 gather_fusion
  100.8 1.5 convolution_select_fusion.4
  102.4 4.5 scatter_fusion
  106.9 0.7 compare_and_fusion.4
  107.6 2.2 gather_fusion
  109.8 1.6 convolution_select_fusion.4
  111.5 4.5 scatter_fusion
  115.9 2.8 convert_element_type.24
  118.9 87.6 %reduce-scatter.3.cloned.1.call-done = bf16[128,256]{1,0:T(8,128)(2,1)} async-done(((bf16[2048,256]{1,0:T(8,128)(2,1)}), bf16[128,256]{1,0:T(8,128)(2,1)}) %reduce-scatter.3.cloned.1.call-update) | async-done | bytes 65552 | tf_op jit(solution)/shard_map/reduce_scatter | solution.py:60
  206.5 1.7 multiply_convert_fusion
  208.2 1.8 fusion.12
  210.0 0.8 convolution_convert_fusion
  210.9 2.8 copy.10
  213.7 126.2 %all-reduce.3.cloned.1.call-done = f32[256,256]{1,0:T(8,128)} async-done(((f32[256,256]{1,0:T(8,128)}), f32[256,256]{1,0:T(8,128)}) %all-reduce.3.cloned.1.call-update) | async-done | bytes 262160 | tf_op jit(solution)/shard_map/psum | solution.py:46
  340.0 73.8 %all-gather.5.cloned.1.call-done = bf16[2048,256]{1,0:T(8,128)(2,1)} async-done(((bf16[128,256]{1,0:T(8,128)(2,1)}), bf16[2048,256]{1,0:T(8,128)(2,1)}) %all-gather.5.cloned.1.call-update) | async-done | bytes 1048592 | tf_op jit(solution)/shard_map/all_gather | solution.py:71
  413.8 2.4 broadcast_in_dim.59
  416.2 34.6 %while.21 = (s32[]{:T(128)}, f32[32,128,256]{2,1,0:T(8,128)}, s32[]{:T(128)}, s32[96]{0:T(128)S(1)}, s32[]{:T(128)}, /*index=5*/bf16[96,128,128]{1,2,0:T(8,128)(...) while((s32[]{:T(128)}, f32[32,128,256]{2,1,0:T(8,128)}, ...), condition=%wide.region_8.9_spmd, body=%wide.region_6.8_spmd.sunk | while | flops 135791792 | bytes 12063415 | solution.py:40
  416.2 0.7 compare_and_fusion.5
  417.0 1.8 gather_fusion.1
  418.8 1.6 convolution_select_fusion.5
  420.5 4.3 scatter_fusion.1
  425.5 1.8 gather_fusion.1
  427.4 1.6 convolution_select_fusion.5
  429.0 4.4 scatter_fusion.1
  434.2 1.8 gather_fusion.1
  436.0 1.6 convolution_select_fusion.5
  437.7 4.5 scatter_fusion.1
  442.9 1.8 gather_fusion.1
  444.8 1.6 convolution_select_fusion.5
  446.4 4.5 scatter_fusion.1
  450.9 2.5 convert_element_type.30
  453.4 3.0 copy.15
  456.3 92.0 %all-reduce.5.cloned.1.call-done = f32[256,256]{1,0:T(8,128)} async-done(((f32[256,256]{1,0:T(8,128)}), f32[256,256]{1,0:T(8,128)}) %all-reduce.5.cloned.1.call-update) | async-done | bytes 262160 | tf_op jit(solution)/shard_map/psum | solution.py:47
  548.4 1.7 broadcast_multiply_fusion
  550.1 102.3 %reduce-scatter.5.cloned.1.call-done = bf16[4096,8]{0,1:T(8,128)(2,1)} async-done(((bf16[4096,256]{0,1:T(8,128)(2,1)}), bf16[4096,8]{0,1:T(8,128)(2,1)}) %reduce-scatter.5.cloned.1.call-update) | async-done | bytes 65552 | tf_op jit(solution)/shard_map/reduce_scatter | solution.py:77
  (41 shorter events, 3.9 us)
Async XLA Ops:
  7.2 199.3 %copy-start = (bf16[256,256]{1,0:T(8,128)(2,1)S(1)}, bf16[256,256]{1,0:T(8,128)(2,1)}, u32[]{:S(2)}) copy-start(bf16[256,256]{1,0:T(8,128)(2,1)} %param.12) | copy-start | bytes 393220
  7.2 67.2 %all-gather.3.cloned.1.call-start = ((), (), s32[]{:S(2)}) async-start(), calls=%async_computation.2 | async-start | bytes 2162688 | tf_op jit(solution)/shard_map/all_gather | solution.py:56
  7.9 198.6 %reduce-scatter.3.cloned.1.call-start = ((), (), s32[]{:S(2)}) async-start(), calls=%async_computation.3 | async-start | bytes 1114112 | tf_op jit(solution)/shard_map/reduce_scatter | solution.py:60
  78.4 1.5 copy-start.2
  78.4 1.5 copy-start.3
  115.9 90.6 %copy-start.4 = (bf16[128,256]{1,0:T(8,128)(2,1)S(1)}, bf16[128,256]{1,0:T(8,128)(2,1)}, u32[]{:S(2)}) copy-start(bf16[128,256]{1,0:T(8,128)(2,1)} %param.17) | copy-start | bytes 196612
  115.9 95.0 %copy-start.1 = (bf16[96,128,128]{2,1,0:T(8,128)(2,1)S(1)}, bf16[96,128,128]{2,1,0:T(8,128)(2,1)}, u32[]{:S(2)}) copy-start(bf16[96,128,128]{2,1,0:T(8,128)(2,1)} %get-tuple-element.329) | copy-start | bytes 9437188
  118.8 221.1 %all-reduce.3.cloned.1.call-start = ((), (), s32[]{:S(2)}) async-start(), calls=%async_computation.4 | async-start | bytes 524288 | tf_op jit(solution)/shard_map/psum | solution.py:46
  210.0 203.8 %all-gather.5.cloned.1.call-start = ((), (), s32[]{:S(2)}) async-start(), calls=%async_computation.6 | async-start | bytes 1114112 | tf_op jit(solution)/shard_map/all_gather | solution.py:71
  210.9 337.5 %all-reduce.5.cloned.1.call-start = ((), (), s32[]{:S(2)}) async-start(), calls=%async_computation.5 | async-start | bytes 524288 | tf_op jit(solution)/shard_map/psum | solution.py:47
  339.9 312.5 %reduce-scatter.5.cloned.1.call-start = ((), (), s32[]{:S(2)}) async-start(), calls=%async_computation.7 | async-start | bytes 2162688 | tf_op jit(solution)/shard_map/reduce_scatter | solution.py:77
Sparse Core Ops, SparseCore 0:
  11.1 63.1 all-gather.2
  118.9 87.5 reduce-scatter.2
  210.6 129.2 all-reduce.2
  342.4 71.3 all-gather.4
  415.9 132.4 all-reduce.4
  553.9 98.4 reduce-scatter.4
